TPU v7x, 32 devices: a whole 2x2x4 slice. The times are simulated.
32 devices in a mesh: dp: 8 (over z, y), tensor: 4 (over x, core).
Axes of the slice: x: 2, y: 2, z: 4, core: 2. Of those that a mesh axis runs over, the one named last changes fastest.
Arguments:
- tokens: bfloat16 [8, 4, 512, 768], P(None, 'tensor', 'dp'), may hold values from -6 to 6
- cotangent: bfloat16 [8, 2048, 768], P('dp', 'tensor'), may hold values from -6 to 6
- lengths: int32 [8], replicated, may hold values from 1 to 2048, 12288 in all
- dealt_to: int32 [8], replicated, may hold values from 0 to 7, each once
- adapter_id: int32 [8], replicated, may hold values from 0 to 7
- norm_gain: bfloat16 [768], replicated, may hold values from 0.25 to 1.75
- w_zx: bfloat16 [768, 2, 1536], P('dp', None, 'tensor'), may hold values from -0.21875 to 0.21875
- w_dt: bfloat16 [768, 24], P('dp', 'tensor'), may hold values from -0.21875 to 0.21875
- w_bc: bfloat16 [768, 256], P('dp'), may hold values from -0.21875 to 0.21875
- x_kernel: float32 [4, 1536], P(None, 'tensor'), may hold values from -3 to 3
- x_offset: float32 [1536], P('tensor'), may hold values from -0.5 to 0.5
- bc_kernel: float32 [4, 256], replicated, may hold values from -3 to 3
- bc_offset: float32 [256], replicated, may hold values from -0.5 to 0.5
- dt_bias: float32 [24], P('tensor'), may hold values from -6.9 to -2.3
- a_log: float32 [24], P('tensor'), may hold values from 0 to 2.77
- d_skip: float32 [24], P('tensor'), may hold values from 0.5 to 1.5
- out_gain: bfloat16 [1536], P('tensor'), may hold values from 0.25 to 1.75
- w_out: bfloat16 [1536, 768], P('tensor', 'dp'), may hold values from -0.15625 to 0.15625
- inlet_down: bfloat16 [8, 768, 16], replicated, may hold values from -0.21875 to 0.21875
- inlet_up: bfloat16 [8, 16, 2, 1536], P(None, None, None, 'tensor'), may hold values from -1.5 to 1.5
- outlet_down: bfloat16 [8, 1536, 16], replicated, may hold values from -0.15625 to 0.15625
- outlet_up: bfloat16 [8, 16, 768], replicated, may hold values from -1.5 to 1.5
Outputs:
- output: bfloat16 [8, 2048, 768], P('dp', 'tensor')
- token_grads: bfloat16 [8, 4, 512, 768], P(None, 'tensor', 'dp')
- inlet_dgrad: float32 [8, 768, 16], replicated
- inlet_ugrad: float32 [8, 16, 2, 1536], P(None, None, None, 'tensor')
- outlet_dgrad: float32 [8, 1536, 16], replicated
- outlet_ugrad: float32 [8, 16, 768], replicated
Inputs may be any that keep to these rules, and one draw needn't show every extreme that they name: `lengths`: the longest sequence has exactly 2048 positions. `dealt_to`: every group is named by exactly one sequence.
All inputs are finite; a program needn't handle non-finite values.
Results may differ from a plain program's by a relative error of at most 0.0085.
Values may be sent and summed in bfloat16 or wider, within the bound.
A program may use at most 128 MiB of HBM per device.

v0:
```python
from functools import partial
import jax
import jax.numpy as jnp
from jax import lax
from jax.sharding import PartitionSpec as P

INNER = 1536
SPAN = 256
ADAPTERS = 8
EPSILON = 1e-05
HIGHEST = lax.Precision.HIGHEST


def causal_conv(values, kernel, offsets):
    kernel_width = kernel.shape[0]
    length = values.shape[0]
    padded = jnp.pad(values, ((kernel_width - 1, 0), (0, 0)))
    running = jnp.zeros_like(values) + offsets[None, :]
    for offset in range(kernel_width):
        running = running + kernel[offset][None, :] * padded[offset : offset + length]
    return running


def state_mixer(heads_x, step_size, decay_rates, input_b, input_c):
    length, head_count, head_dim = heads_x.shape
    blocks = length // SPAN
    state_dim = input_b.shape[1]
    block_x = heads_x.reshape(blocks, SPAN, head_count, head_dim)
    block_dt = step_size.reshape(blocks, SPAN, head_count)
    block_b = input_b.reshape(blocks, SPAN, state_dim)
    block_c = input_c.reshape(blocks, SPAN, state_dim)
    causal = jnp.arange(SPAN)[:, None] >= jnp.arange(SPAN)[None, :]
    within = jnp.einsum(
        "ts,csh->cth",
        causal.astype(jnp.float32),
        block_dt * decay_rates[None, None, :],
        precision=HIGHEST,
    )
    scores = jnp.einsum("ctn,csn->cts", block_c, block_b, precision=HIGHEST)
    causal_full = causal[None, :, :, None]
    spread = within[:, :, None, :] - within[:, None, :, :]
    mixing = jnp.where(causal_full, jnp.exp(jnp.where(causal_full, spread, 0.0)), 0.0)
    weights = scores[:, :, :, None] * mixing * block_dt[:, None, :, :]
    inside = jnp.einsum("ctsh,cshp->cthp", weights, block_x, precision=HIGHEST)
    span_total = within[:, -1, :]
    tail_weight = jnp.exp(span_total[:, None, :] - within) * block_dt
    fresh_state = jnp.einsum("cth,cthp,ctn->chpn", tail_weight, block_x, block_b, precision=HIGHEST)
    span_ids = jnp.arange(blocks)
    through = jnp.einsum(
        "dc,ch->dh",
        (span_ids[:, None] >= span_ids[None, :]).astype(jnp.float32),
        span_total,
        precision=HIGHEST,
    )
    before = through - span_total
    earlier = (span_ids[:, None] > span_ids[None, :])[:, :, None]
    passing = jnp.where(
        earlier, jnp.exp(jnp.where(earlier, before[:, None, :] - through[None, :, :], 0.0)), 0.0
    )
    state_in = jnp.einsum("dch,chpn->dhpn", passing, fresh_state, precision=HIGHEST)
    carried = (
        jnp.einsum("ctn,chpn->cthp", block_c, state_in, precision=HIGHEST)
        * jnp.exp(within)[:, :, :, None]
    )
    return (inside + carried).reshape(length, head_count, head_dim)


def mixer_part(weights_local, p_zx, p_bc, p_dt):
    x_kernel, x_offset, bc_kernel, bc_offset, dt_bias, a_log, d_skip = weights_local
    length = p_zx.shape[0]
    inner_local = p_zx.shape[2]
    head_count = p_dt.shape[1]
    state_dim = p_bc.shape[1] // 2
    inner_x = jax.nn.silu(causal_conv(p_zx[:, 1, :], x_kernel, x_offset))
    mixed_bc = jax.nn.silu(causal_conv(p_bc, bc_kernel, bc_offset))
    step_size = jax.nn.softplus(p_dt + dt_bias)
    heads_x = inner_x.reshape(length, head_count, inner_local // head_count)
    mixed = state_mixer(
        heads_x, step_size, -jnp.exp(a_log), mixed_bc[:, :state_dim], mixed_bc[:, state_dim:]
    )
    mixed = mixed + d_skip[None, :, None] * heads_x
    return mixed.reshape(length, inner_local) * jax.nn.silu(p_zx[:, 0, :])


def shards(
    tokens,
    cotangent,
    lengths,
    dealt_to,
    adapter_id,
    norm_gain,
    w_zx,
    w_dt,
    w_bc,
    x_kernel,
    x_offset,
    bc_kernel,
    bc_offset,
    dt_bias,
    a_log,
    d_skip,
    out_gain,
    w_out,
    inlet_down,
    inlet_up,
    outlet_down,
    outlet_up,
):
    model_dim = tokens.shape[3]
    inner_local = w_zx.shape[2]
    full_zx, full_dt, full_bc, full_out = (
        lax.all_gather(w_zx, "dp", axis=0, tiled=True),
        lax.all_gather(w_dt, "dp", axis=0, tiled=True),
        lax.all_gather(w_bc, "dp", axis=0, tiled=True),
        lax.all_gather(w_out, "dp", axis=1, tiled=True),
    )
    seq_count = dealt_to.shape[0]
    slot_ids = jnp.arange(seq_count, dtype=jnp.int32)
    placed = (dealt_to[None, :] == slot_ids[:, None]).astype(jnp.int32)
    seq_of = jnp.sum(placed * slot_ids[None, :], axis=1)
    picked = jnp.take(tokens, seq_of, axis=0)
    arrived = lax.all_to_all(picked, "dp", split_axis=0, concat_axis=2, tiled=True)
    tok_rows = arrived.reshape(-1, model_dim)
    tok_dev = tok_rows.shape[0]
    group_id = lax.axis_index("dp")
    own_seq = jnp.take(seq_of, group_id)
    chosen = (jnp.arange(ADAPTERS, dtype=jnp.int32) == jnp.take(adapter_id, own_seq)).astype(
        jnp.float32
    )
    positions = lax.axis_index("tensor") * tok_dev + jnp.arange(tok_dev, dtype=jnp.int32)
    valid_rows = (positions < jnp.take(lengths, own_seq)).astype(jnp.float32)[:, None]

    def select_one(stacked):
        return jnp.einsum("k,k...->...", chosen, stacked.astype(jnp.float32)).astype(jnp.bfloat16)

    in_down = select_one(inlet_down)
    in_up = select_one(inlet_up)
    out_down = select_one(outlet_down)
    out_up = select_one(outlet_up)
    residual = tok_rows.astype(jnp.float32)
    gain_in = norm_gain.astype(jnp.float32)
    inv_in = lax.rsqrt(jnp.mean(residual * residual, axis=1, keepdims=True) + EPSILON)
    normed = (residual * inv_in * gain_in).astype(jnp.bfloat16)
    hidden_in = jnp.dot(normed, in_down, preferred_element_type=jnp.float32).astype(jnp.bfloat16)
    all_normed, all_hidden = (
        lax.all_gather(normed, "tensor", axis=0, tiled=True),
        lax.all_gather(hidden_in, "tensor", axis=0, tiled=True),
    )
    zx_matrix = full_zx.reshape(model_dim, 2 * inner_local)
    up_matrix = in_up.reshape(in_up.shape[0], 2 * inner_local)
    p_zx = jnp.dot(all_normed, zx_matrix, preferred_element_type=jnp.float32) + jnp.dot(
        all_hidden, up_matrix, preferred_element_type=jnp.float32
    )
    p_zx = p_zx.reshape(-1, 2, inner_local)
    p_bc = jnp.dot(all_normed, full_bc, preferred_element_type=jnp.float32)
    p_dt = jnp.dot(all_normed, full_dt, preferred_element_type=jnp.float32)
    mixer_weights = (x_kernel, x_offset, bc_kernel, bc_offset, dt_bias, a_log, d_skip)
    gated_act, mixer_pull = jax.vjp(partial(mixer_part, mixer_weights), p_zx, p_bc, p_dt)
    gain_rows = out_gain.astype(jnp.float32)
    squares = lax.psum(jnp.sum(gated_act * gated_act, axis=1), "tensor")
    inv_out = lax.rsqrt(squares / INNER + EPSILON)[:, None]
    normed_out = (gated_act * inv_out * gain_rows).astype(jnp.bfloat16)
    row_start = lax.axis_index("tensor") * inner_local
    down_rows = lax.dynamic_slice_in_dim(out_down, row_start, inner_local, 0)
    summed_out, summed_hidden = (
        lax.psum_scatter(
            jnp.dot(normed_out, full_out, preferred_element_type=jnp.float32),
            "tensor",
            scatter_dimension=0,
            tiled=True,
        ),
        lax.psum_scatter(
            jnp.dot(normed_out, down_rows, preferred_element_type=jnp.float32),
            "tensor",
            scatter_dimension=0,
            tiled=True,
        ),
    )
    hidden_out = summed_hidden.astype(jnp.bfloat16)
    branch_out = summed_out + jnp.dot(hidden_out, out_up, preferred_element_type=jnp.float32)
    output = (
        (residual + valid_rows * branch_out).astype(jnp.bfloat16).reshape(1, tok_dev, model_dim)
    )
    cot_rows = cotangent.reshape(tok_dev, model_dim).astype(jnp.float32)
    grad_branch = (cot_rows * valid_rows).astype(jnp.bfloat16)
    back_hidden = jnp.dot(grad_branch, out_up.T, preferred_element_type=jnp.float32).astype(
        jnp.bfloat16
    )
    outup_sum = jnp.dot(hidden_out.T, grad_branch, preferred_element_type=jnp.float32)
    wide_branch, wide_hidden = (
        lax.all_gather(grad_branch, "tensor", axis=0, tiled=True),
        lax.all_gather(back_hidden, "tensor", axis=0, tiled=True),
    )
    back_normed = jnp.dot(wide_branch, full_out.T, preferred_element_type=jnp.float32) + jnp.dot(
        wide_hidden, down_rows.T, preferred_element_type=jnp.float32
    )
    weighted_out = gain_rows * back_normed
    cross_sum = lax.psum(jnp.sum(weighted_out * gated_act, axis=1), "tensor")
    back_gated = inv_out * weighted_out - gated_act * inv_out**3 * (cross_sum / INNER)[:, None]
    local_rows = jnp.dot(normed_out.T, wide_hidden, preferred_element_type=jnp.float32)
    outdown_sum = lax.dynamic_update_slice_in_dim(
        jnp.zeros((INNER, local_rows.shape[1]), jnp.float32), local_rows, row_start, 0
    )
    grad_zx, grad_bc, grad_dt = mixer_pull(back_gated)
    low_zx3 = grad_zx.astype(jnp.bfloat16)
    low_zx = low_zx3.reshape(-1, 2 * inner_local)
    low_dt = grad_dt.astype(jnp.bfloat16)
    inup_sum = jnp.dot(all_hidden.T, low_zx, preferred_element_type=jnp.float32).reshape(
        -1, 2, inner_local
    )
    normed_part = jnp.dot(low_zx, zx_matrix.T, preferred_element_type=jnp.float32) + jnp.dot(
        low_dt, full_dt.T, preferred_element_type=jnp.float32
    )
    hidden_part = jnp.dot(low_zx, up_matrix.T, preferred_element_type=jnp.float32)
    grad_normed, grad_hidden, grad_bcrows = (
        lax.psum_scatter(normed_part, "tensor", scatter_dimension=0, tiled=True),
        lax.psum_scatter(hidden_part, "tensor", scatter_dimension=0, tiled=True),
        lax.psum_scatter(grad_bc, "tensor", scatter_dimension=0, tiled=True),
    )
    low_bc = grad_bcrows.astype(jnp.bfloat16)
    low_hidden = grad_hidden.astype(jnp.bfloat16)
    grad_normed = (
        grad_normed
        + jnp.dot(low_bc, full_bc.T, preferred_element_type=jnp.float32)
        + jnp.dot(low_hidden, in_down.T, preferred_element_type=jnp.float32)
    )
    indown_sum = jnp.dot(normed.T, low_hidden, preferred_element_type=jnp.float32)
    weighted = gain_in * grad_normed
    grad_input = (
        cot_rows
        + inv_in * weighted
        - residual * inv_in**3 * jnp.mean(weighted * residual, axis=1, keepdims=True)
    )
    sent_back = grad_input.astype(jnp.bfloat16).reshape(1, 1, tok_dev, model_dim)
    returned = lax.all_to_all(sent_back, "dp", split_axis=2, concat_axis=0, tiled=True)
    token_grads = jnp.take(returned, dealt_to, axis=0)
    inlet_dgrad, outlet_dgrad, outlet_ugrad = lax.psum(
        (
            chosen[:, None, None] * indown_sum[None],
            chosen[:, None, None] * outdown_sum[None],
            chosen[:, None, None] * outup_sum[None],
        ),
        ("dp", "tensor"),
    )
    inlet_ugrad = lax.psum(
        (chosen[:, None, None, None] * inup_sum[None]).astype(jnp.bfloat16), "dp"
    ).astype(jnp.float32)
    return (output, token_grads, inlet_dgrad, inlet_ugrad, outlet_dgrad, outlet_ugrad)


def solution(mesh):
    in_specs = (
        P(None, "tensor", "dp", None),
        P("dp", "tensor", None),
        P(),
        P(),
        P(),
        P(),
        P("dp", None, "tensor"),
        P("dp", "tensor"),
        P("dp", None),
        P(None, "tensor"),
        P("tensor"),
        P(),
        P(),
        P("tensor"),
        P("tensor"),
        P("tensor"),
        P("tensor"),
        P("tensor", "dp"),
        P(),
        P(None, None, None, "tensor"),
        P(),
        P(),
    )
    out_specs = (
        P("dp", "tensor", None),
        P(None, "tensor", "dp", None),
        P(),
        P(None, None, None, "tensor"),
        P(),
        P(),
    )
    return jax.shard_map(shards, mesh=mesh, in_specs=in_specs, out_specs=out_specs, check_vma=False)
```

profile of v0, /device:TPU:0, one launch (start us, length us, event | category | flops | bytes accessed | tf_op | source)
XLA Modules:
  0.0 787.3 jit_solution(1121650660833322522)
XLA Ops:
  17.4 7.4 all-to-all-start
  24.9 26.5 %all-to-all-done = bf16[8,1,64,768]{3,2,1,0:T(8,128)(2,1)S(1)} async-done(((bf16[8,1,64,768]{3,2,1,0:T(8,128)(2,1)}), bf16[8,1,64,768]{3,2,1,0:T(8,128)(2,1)S(1)}, u32[]{:S(2)}, u32[]{:S(2)}) %all-to-all-start) | async-done | bytes 786464 | tf_op jit(solution)/shard_map/all_to_all | solution.py:122
  56.1 26.0 %all-gather = bf16[8,96,6]{1,2,0:T(8,128)(2,1)S(1)} all-gather(bf16[1,96,6]{1,2,0:T(8,128)(2,1)S(1)} %bitcast.353), channel_id=1, replica_groups=mesh['dp'=8,'tensor'=4] {'dp'}, dimensions={0}, use_global_device_ids=true | all-gather | bytes 10368 | tf_op jit(solution)/shard_map/all_gather | solution.py:113
  85.3 5.8 all_gather.31
  93.0 31.3 %all_gather.27 = bf16[768,256]{1,0:T(8,128)(2,1)S(1)} all-gather(bf16[96,256]{1,0:T(8,128)(2,1)} %param.32), channel_id=1, replica_groups=mesh['dp'=8,'tensor'=4] {'dp'}, dimensions={0}, use_global_device_ids=true | all-gather | bytes 442368 | tf_op jit(solution)/shard_map/all_gather | solution.py:114
  126.0 31.6 %all_gather.29 = bf16[384,768]{0,1:T(8,128)(2,1)S(1)} all-gather(bf16[384,96]{0,1:T(8,128)(2,1)} %param.41), channel_id=1, replica_groups=mesh['dp'=8,'tensor'=4] {'dp'}, dimensions={1}, use_global_device_ids=true | all-gather | bytes 663552 | tf_op jit(solution)/shard_map/all_gather | solution.py:115
  158.0 5.9 all_gather.26
  166.2 5.4 fusion.223
  171.6 3.6 compare_select_fusion.2
  186.2 3.9 fusion.219
  191.2 3.0 fusion.215
  194.2 3.6 copy.268
  202.9 3.8 copy.269
  206.7 4.4 fusion.33
  211.1 4.0 copy.197
  215.1 3.5 copy.271
  220.5 3.8 fusion.41
  226.8 3.0 fusion.84
  229.9 15.3 %bitcast_add_fusion.2 = f32[8,256,6,64]{1,3,2,0:T(8,128)S(1)} fusion(f32[8,256,6,64]{1,3,2,0:T(8,128)S(1)} %fusion.84, f32[8,256,6]{1,2,0:T(8,128)S(1)} %bitcast.332, f32[8,256,6]{1,2,0:T(8,128)S(1)} %copy-done.64, f32[8,256,256]{2,1,0:T(8,128)S(1)} %fusion.221, pred[256,256]{1,0:T(8,128)(4,1)S(1)} %copy-done.65, f32[8,256,6,64]{1,0,3,2:T(8,128)S(1)} %bitcast.297, ...), kind=kOutput, calls=%fused_computation.50 | convolution fusion | flops 2433220608 | bytes 11747328 | tf_op jit(solution)/shard_map/jvp(ctsh,cshp->cthp)/dot_general | solution.py:44
  250.1 3.6 copy.213
  253.6 10.0 %multiply_reduce_fusion.3 = (f32[2048]{0:T(1024)}, f32[2048]{0:T(1024)}, f32[2048,384]{1,0:T(8,128)}, f32[2048,384]{1,0:T(8,128)}) fusion(f32[2048,1,384]{2,0,1:T(8,128)} %copy.269, f32[2048,384]{1,0:T(8,128)} %copy.213, f32[2048,384]{1,0:T(8,128)} %get-tuple-element.75, f32[384]{0:T(512)} %mul.552, f32[2048,384]{1,0:T(8,128)} %fusion.223, ...), kind=kOutput, calls=%fused_computation.55 | convolution fusion | flops 38531072 | bytes 19058692 | tf_op jit(solution)/shard_map/dot_general | solution.py:194
  263.6 13.0 %all-reduce.16 = (f32[2048]{0:T(1024)}, f32[2048]{0:T(1024)}) all-reduce(f32[2048]{0:T(1024)} %get-tuple-element.57, f32[2048]{0:T(1024)} %get-tuple-element.56), channel_id=1, replica_groups=mesh['dp'=8,'tensor'=4] {'tensor'}, use_global_device_ids=true, to_apply=%region_3.5 | all-reduce | flops 4096 | bytes 32768 | tf_op jit(solution)/shard_map/psum | solution.py:160
  277.3 9.0 %fusion.24 = (f32[2048,1,384]{2,0,1:T(8,128)}, f32[2048,384]{1,0:T(8,128)}, bf16[2048,384]{1,0:T(8,128)(2,1)}) fusion(f32[2048,1,384]{2,0,1:T(8,128)} %copy.269, f32[2048]{0:T(1024)S(1)} %get-tuple-element.106, f32[2048,384]{1,0:T(8,128)} %get-tuple-element.73, f32[2048]{0:T(1024)S(1)} %get-tuple-element.93, f32[2048,384]{1,0:T(8,128)} %get-tuple-element.103, ...), kind=kLoop, calls=%fused_computation.34 | loop fusion | flops 19660800 | bytes 23620608 | tf_op jit(solution)/shard_map/transpose(jvp())/broadcast_in_dim | solution.py:82
  286.3 4.0 copy.215
  290.3 3.4 copy.274
  293.8 7.0 fusion.88
  300.8 3.8 fusion.76
  304.6 5.9 fusion.211
  313.0 7.0 fusion.91
  320.0 4.5 fusion.78
  325.3 24.8 %fusion.9 = (f32[8,256,6]{1,2,0:T(8,128)}, f32[8,256,6]{1,2,0:T(8,128)}, f32[8,256,6]{1,2,0:T(8,128)}, f32[8,256,256]{2,1,0:T(8,128)S(1)}) fusion(f32[8,256,6]{1,2,0:T(8,128)} %bitcast.330, f32[8,256,6]{1,2,0:T(8,128)} %copy.199, f32[8,256,256]{2,1,0:T(8,128)} %copy-done.32, pred[256,256]{1,0:T(8,128)(4,1)} %iota_compare_fusion, ...), kind=kOutput, calls=%fused_computation.14 | convolution fusion | flops 2462543872 | bytes 10797056 | tf_op jit(solution)/shard_map/transpose(jvp(ctsh,cshp->cthp))/dot_general | solution.py:44
  350.0 3.5 convolution_add_fusion.2
  359.2 14.2 %bitcast_add_fusion.1 = f32[8,256,6,64]{1,3,2,0:T(8,128)S(1)} fusion(f32[8,256,6,64]{1,3,2,0:T(8,128)} %fusion.78, f32[8,256,6]{1,2,0:T(8,128)} %bitcast.331, f32[8,256,6]{1,2,0:T(8,128)} %copy.199, f32[8,256,256]{2,1,0:T(8,128)} %copy-done.32, pred[256,256]{1,0:T(8,128)(4,1)} %iota_compare_fusion, f32[8,6,64,256]{3,0,2,1:T(8,128)} %bitcast.304, ...), kind=kOutput, calls=%fused_computation.43 | convolution fusion | flops 2433220608 | bytes 11747328 | tf_op jit(solution)/shard_map/transpose(jvp(ctsh,cshp->cthp))/dot_general | solution.py:44
  375.1 3.1 copy.275
  378.3 3.7 copy.222
  382.1 3.8 multiply_reduce_fusion.1
  387.8 4.3 multiply_reduce_fusion.2
  394.0 3.2 broadcast_multiply_fusion
  402.2 4.0 fusion.224
  406.2 3.8 bitcast_add_fusion
  420.0 4.5 fusion.222
  428.5 50.1 %reduce-scatter.10.cloned.1.call-done = f32[512,768]{1,0:T(8,128)} async-done(((f32[2048,768]{1,0:T(8,128)}), f32[512,768]{1,0:T(8,128)}) %reduce-scatter.10.cloned.1.call-update) | async-done | bytes 1572880 | tf_op jit(solution)/shard_map/reduce_scatter | solution.py:216
  484.2 6.5 reduce.13
  491.8 5.7 all-to-all-start.1
  497.5 3.9 reduce-scatter.8.cloned.1.call-done
  504.4 70.8 %all-reduce.20.cloned.1.call-done = bf16[8,16,2,384]{3,2,1,0:T(2,128)(2,1)} async-done(((bf16[8,16,2,384]{3,2,1,0:T(2,128)(2,1)}), bf16[8,16,2,384]{3,2,1,0:T(2,128)(2,1)}) %all-reduce.20.cloned.1.call-update) | async-done | bytes 196624 | tf_op jit(solution)/shard_map/psum | solution.py:245
  577.0 58.3 %reduce-scatter.6.cloned.1.call-done = f32[512,768]{1,0:T(8,128)} async-done(((f32[2048,768]{1,0:T(8,128)}), f32[512,768]{1,0:T(8,128)}) %reduce-scatter.6.cloned.1.call-update) | async-done | bytes 1572880 | tf_op jit(solution)/shard_map/reduce_scatter | solution.py:166
  640.6 133.8 %all-reduce.22.cloned.1.call-done = (f32[8,768,16]{1,2,0:T(8,128)}, f32[8,1536,16]{1,2,0:T(8,128)}, f32[8,16,768]{2,1,0:T(8,128)}) async-done(((f32[8,768,16]{1,2,0:T(8,128)}, f32[8,1536,16]{1,2,0:T(8,128)}, f32[8,16,768]{2,1,0:T(8,128)}), (f32[8,768,16]{1,2,0:T(8,128)}, f32[8,1536,16]{1,2,0:T(8,128)}, f32[8,16,768]{2,1,0:T(8,128)})) %all-reduce.22.cloned.1.call-update) | async-done | bytes 1572880 | tf_op jit(solution)/shard_map/psum | solution.py:237
  (340 shorter events, 104.4 us)
Async XLA Ops:
  7.2 156.6 %all-gather.7.cloned.1.call-start = ((), (), s32[]{:S(2)}) async-start(), calls=%async_computation.8 | async-start | bytes 1327104 | tf_op jit(solution)/shard_map/all_gather | solution.py:112
  8.9 157.3 %all-gather.9.cloned.1.call-start = ((), (), s32[]{:S(2)}) async-start(), calls=%async_computation.11 | async-start | bytes 3932160 | tf_op jit(solution)/shard_map/all_gather | solution.py:191
  15.6 9.3 %copy-start.94 = (bf16[768]{0:T(1024)(128)(2,1)S(1)}, bf16[768]{0:T(1024)(128)(2,1)}, u32[]{:S(2)}) copy-start(bf16[768]{0:T(1024)(128)(2,1)} %param.29) | copy-start | bytes 4612
  16.3 37.2 %copy-start.100 = (s32[8]{0:T(128)S(1)}, s32[8]{0:T(128)}, u32[]{:S(2)}) copy-start(s32[8]{0:T(128)} %param.28) | copy-start | bytes 100
  16.3 38.5 %copy-start.97 = (bf16[384]{0:T(512)(128)(2,1)S(1)}, bf16[384]{0:T(512)(128)(2,1)}, u32[]{:S(2)}) copy-start(bf16[384]{0:T(512)(128)(2,1)} %param.40) | copy-start | bytes 2308
  16.3 39.1 %copy-start.98 = (f32[6]{0:T(128)S(1)}, f32[6]{0:T(128)}, u32[]{:S(2)}) copy-start(f32[6]{0:T(128)} %param.39) | copy-start | bytes 76
  16.4 39.8 %copy-start.95 = (bf16[96,6]{0,1:T(8,128)(2,1)S(1)}, bf16[96,6]{0,1:T(8,128)(2,1)}, u32[]{:S(2)}) copy-start(bf16[96,6]{0,1:T(8,128)(2,1)} %param.31) | copy-start | bytes 3460
  16.4 65.9 %copy-start.55 = (bf16[8,16,2,384]{3,2,1,0:T(2,128)(2,1)S(1)}, bf16[8,16,2,384]{3,2,1,0:T(2,128)(2,1)}, u32[]{:S(2)}) copy-start(bf16[8,16,2,384]{3,2,1,0:T(2,128)(2,1)} %param.43) | copy-start | bytes 589828
  16.4 66.7 %copy-start.56 = (bf16[8,768,16]{1,2,0:T(8,128)(2,1)S(1)}, bf16[8,768,16]{1,2,0:T(8,128)(2,1)}, u32[]{:S(2)}) copy-start(bf16[8,768,16]{1,2,0:T(8,128)(2,1)} %param.42) | copy-start | bytes 589828
  17.4 66.1 %copy-start.48 = (bf16[8,1536,16]{1,2,0:T(8,128)(2,1)S(1)}, bf16[8,1536,16]{1,2,0:T(8,128)(2,1)}, u32[]{:S(2)}) copy-start(bf16[8,1536,16]{1,2,0:T(8,128)(2,1)} %param.44) | copy-start | bytes 1179652
  17.4 67.4 %copy-start.57 = (bf16[8,16,768]{2,1,0:T(8,128)(2,1)S(1)}, bf16[8,16,768]{2,1,0:T(8,128)(2,1)}, u32[]{:S(2)}) copy-start(bf16[8,16,768]{2,1,0:T(8,128)(2,1)} %param.45) | copy-start | bytes 589828
  17.4 67.6 %copy-start.19 = (bf16[512,768]{1,0:T(8,128)(2,1)S(1)}, bf16[512,768]{1,0:T(8,128)(2,1)}, u32[]{:S(2)}) copy-start(bf16[512,768]{1,0:T(8,128)(2,1)} %fusion.62) | copy-start | bytes 2359300
  17.4 34.0 %all-to-all-start = ((bf16[8,1,64,768]{3,2,1,0:T(8,128)(2,1)}), bf16[8,1,64,768]{3,2,1,0:T(8,128)(2,1)S(1)}, u32[]{:S(2)}, u32[]{:S(2)}) async-start(bf16[8,1,64,768]{3,2,1,0:T(8,128)(2,1)} %bitcast_select_fusion.1), calls=%async_computation | async-start | bytes 1572864 | tf_op jit(solution)/shard_map/all_to_all | solution.py:122
  24.8 66.9 %copy-start.90 = (f32[4,384]{1,0:T(4,128)S(1)}, f32[4,384]{1,0:T(4,128)}, u32[]{:S(2)}) copy-start(f32[4,384]{1,0:T(4,128)} %param.33) | copy-start | bytes 18436
  24.8 146.8 %all-gather.5.cloned.1.call-start = ((), (), s32[]{:S(2)}) async-start(), calls=%async_computation.7 | async-start | bytes 3932160 | tf_op jit(solution)/shard_map/all_gather | solution.py:146
  24.9 26.9 %copy-start.66 = (f32[768]{0:T(1024)}, f32[768]{0:T(1024)S(1)}, u32[]{:S(2)}) copy-start(f32[768]{0:T(1024)S(1)} %convert_element_type.111) | copy-start | bytes 9220
  51.5 40.9 %copy-start.5 = (bf16[8,1,64,768]{3,2,1,0:T(8,128)(2,1)}, bf16[8,1,64,768]{3,2,1,0:T(8,128)(2,1)S(1)}, u32[]{:S(2)}) copy-start(bf16[8,1,64,768]{3,2,1,0:T(8,128)(2,1)S(1)} %all-to-all-done) | copy-start | bytes 2359300
  51.7 73.8 %copy-start.91 = (f32[4,256]{1,0:T(4,128)S(1)}, f32[4,256]{1,0:T(4,128)}, u32[]{:S(2)}) copy-start(f32[4,256]{1,0:T(4,128)} %param.35) | copy-start | bytes 12292
  53.5 104.2 %copy-start.21 = (bf16[512,768]{1,0:T(8,128)(2,1)S(1)}, bf16[512,768]{1,0:T(8,128)(2,1)}, u32[]{:S(2)}) copy-start(bf16[512,768]{1,0:T(8,128)(2,1)} %fusion.67) | copy-start | bytes 2359300
  53.5 373.6 %reduce-scatter.12.cloned.1.call-start = ((), (), s32[]{:S(2)}) async-start(), calls=%async_computation.13 | async-start | bytes 2621440 | tf_op jit(solution)/shard_map/reduce_scatter | solution.py:218
  83.5 82.7 %copy-start.37 = (bf16[1,768,16]{2,1,0:T(8,128)(2,1)}, bf16[1,768,16]{2,1,0:T(8,128)(2,1)S(1)}, u32[]{:S(2)}) copy-start(bf16[1,768,16]{2,1,0:T(8,128)(2,1)S(1)} %copy.244) | copy-start | bytes 73732
  85.0 40.4 %copy-start.53 = (bf16[1,16,768]{2,0,1:T(2,128)(2,1)}, bf16[1,16,768]{2,0,1:T(2,128)(2,1)S(1)}, u32[]{:S(2)}) copy-start(bf16[1,16,768]{2,0,1:T(2,128)(2,1)S(1)} %fusion.135) | copy-start | bytes 73732
  157.7 14.0 %copy-start.30 = (bf16[384,768]{0,1:T(8,128)(2,1)}, bf16[384,768]{0,1:T(8,128)(2,1)S(1)}, u32[]{:S(2)}) copy-start(bf16[384,768]{0,1:T(8,128)(2,1)S(1)} %all_gather.29) | copy-start | bytes 1769476
  171.6 14.5 %copy-start.3 = (bf16[2048,768]{1,0:T(8,128)(2,1)S(1)}, bf16[2048,768]{1,0:T(8,128)(2,1)}, u32[]{:S(2)}) copy-start(bf16[2048,768]{1,0:T(8,128)(2,1)} %all-gather.5.cloned.1.call-done) | copy-start | bytes 9437188
  220.5 9.4 %copy-start.32 = (f32[8,256,256]{2,1,0:T(8,128)}, f32[8,256,256]{2,1,0:T(8,128)S(1)}, u32[]{:S(2)}) copy-start(f32[8,256,256]{2,1,0:T(8,128)S(1)} %fusion.221) | copy-start | bytes 6291460
  229.9 15.4 %copy-start.23 = (f32[8,256,6,64]{1,3,2,0:T(8,128)}, f32[8,256,6,64]{1,3,2,0:T(8,128)S(1)}, u32[]{:S(2)}) copy-start(f32[8,256,6,64]{1,3,2,0:T(8,128)S(1)} %fusion.84) | copy-start | bytes 9437188
  293.7 26.3 %copy-start.2 = (f32[48,8,8,256]{3,2,1,0:T(8,128)}, f32[48,8,8,256]{3,2,1,0:T(8,128)S(1)}, u32[]{:S(2)}) copy-start(f32[48,8,8,256]{3,2,1,0:T(8,128)S(1)} %copy.274) | copy-start | bytes 9437188
  325.3 24.8 %copy-start.14 = (f32[2048,128]{1,0:T(8,128)S(1)}, f32[2048,128]{1,0:T(8,128)}, u32[]{:S(2)}) copy-start(f32[2048,128]{1,0:T(8,128)} %get-tuple-element.90) | copy-start | bytes 3145732
  325.3 24.8 %copy-start.28 = (f32[8,256,128]{2,1,0:T(8,128)S(1)}, f32[8,256,128]{2,1,0:T(8,128)}, u32[]{:S(2)}) copy-start(f32[8,256,128]{2,1,0:T(8,128)} %fusion.91) | copy-start | bytes 3145732
  359.1 69.4 %reduce-scatter.14.cloned.1.call-start = ((), (), s32[]{:S(2)}) async-start(), calls=%async_computation.14 | async-start | bytes 163840 | tf_op jit(solution)/shard_map/reduce_scatter | solution.py:217
  402.1 76.5 %reduce-scatter.10.cloned.1.call-start = ((), (), s32[]{:S(2)}) async-start(), calls=%async_computation.12 | async-start | bytes 7864320 | tf_op jit(solution)/shard_map/reduce_scatter | solution.py:216
  410.0 91.3 %reduce-scatter.8.cloned.1.call-start = ((), (), s32[]{:S(2)}) async-start(), calls=%async_computation.10 | async-start | bytes 163840 | tf_op jit(solution)/shard_map/reduce_scatter | solution.py:172
  415.8 159.3 %all-reduce.20.cloned.1.call-start = ((), (), s32[]{:S(2)}) async-start(), calls=%async_computation.15 | async-start | bytes 393216 | tf_op jit(solution)/shard_map/psum | solution.py:245
  419.9 215.4 %reduce-scatter.6.cloned.1.call-start = ((), (), s32[]{:S(2)}) async-start(), calls=%async_computation.9 | async-start | bytes 7864320 | tf_op jit(solution)/shard_map/reduce_scatter | solution.py:166
  425.1 53.5 %copy-start.6 = (bf16[8,1,64,768]{3,2,1,0:T(8,128)(2,1)S(1)}, bf16[8,1,64,768]{3,2,1,0:T(8,128)(2,1)}, u32[]{:S(2)}) copy-start(bf16[8,1,64,768]{3,2,1,0:T(8,128)(2,1)} %copy-done.5) | copy-start | bytes 2359300
  425.1 53.5 %copy-start.67 = (f32[768]{0:T(1024)S(1)}, f32[768]{0:T(1024)}, u32[]{:S(2)}) copy-start(f32[768]{0:T(1024)} %copy-done.66) | copy-start | bytes 9220
  428.5 52.3 %copy-start.29 = (bf16[1,512,768]{2,1,0:T(8,128)(2,1)S(1)}, bf16[1,512,768]{2,1,0:T(8,128)(2,1)}, u32[]{:S(2)}) copy-start(bf16[1,512,768]{2,1,0:T(8,128)(2,1)} %param.25) | copy-start | bytes 2359300
  483.7 17.7 %copy-start.20 = (bf16[512,768]{1,0:T(8,128)(2,1)S(1)}, bf16[512,768]{1,0:T(8,128)(2,1)}, u32[]{:S(2)}) copy-start(bf16[512,768]{1,0:T(8,128)(2,1)} %fusion.62) | copy-start | bytes 2359300
  484.2 19.0 %copy-start.22 = (bf16[512,768]{1,0:T(8,128)(2,1)S(1)}, bf16[512,768]{1,0:T(8,128)(2,1)}, u32[]{:S(2)}) copy-start(bf16[512,768]{1,0:T(8,128)(2,1)} %fusion.67) | copy-start | bytes 2359300
  484.2 19.0 %copy-start.58 = (f32[512,16]{0,1:T(8,128)S(1)}, f32[512,16]{0,1:T(8,128)}, u32[]{:S(2)}) copy-start(f32[512,16]{0,1:T(8,128)} %reduce-scatter.14.cloned.1.call-done) | copy-start | bytes 98308
  491.7 12.6 %copy-start.99 = (s32[8]{0:T(128)S(1)}, s32[8]{0:T(128)}, u32[]{:S(2)}) copy-start(s32[8]{0:T(128)} %compare_select_fusion.3) | copy-start | bytes 100
  491.7 12.6 %copy-start.102 = (s32[8]{0:T(128)S(1)}, s32[8]{0:T(128)}, u32[]{:S(2)}) copy-start(s32[8]{0:T(128)} %param.27) | copy-start | bytes 100
  491.7 143.6 %copy-start.54 = (bf16[1,16,768]{2,0,1:T(2,128)(2,1)S(1)}, bf16[1,16,768]{2,0,1:T(2,128)(2,1)}, u32[]{:S(2)}) copy-start(bf16[1,16,768]{2,0,1:T(2,128)(2,1)} %copy-done.53) | copy-start | bytes 73732
  491.8 143.6 %copy-start.78 = (f32[512]{0:T(512)S(1)}, f32[512]{0:T(512)}, u32[]{:S(2)}) copy-start(f32[512]{0:T(512)} %copy-done.77) | copy-start | bytes 6148
  491.8 146.3 %all-to-all-start.1 = ((bf16[8,2,24576]{2,1,0:T(2,128)(2,1)}), bf16[8,2,24576]{2,1,0:T(2,128)(2,1)S(1)}, u32[]{:S(2)}, u32[]{:S(2)}) async-start(bf16[8,2,24576]{2,1,0:T(2,128)(2,1)} %reshape.388), calls=%async_computation.6 | async-start | bytes 1572864 | tf_op jit(solution)/shard_map/all_to_all | solution.py:235
  497.4 277.0 %all-reduce.22.cloned.1.call-start = ((), (), s32[]{:S(2)}) async-start(), calls=%async_computation.16 | async-start | bytes 3145728 | tf_op jit(solution)/shard_map/psum | solution.py:237
  501.3 134.0 %copy-start.59 = (f32[512,16]{0,1:T(8,128)S(1)}, f32[512,16]{0,1:T(8,128)}, u32[]{:S(2)}) copy-start(f32[512,16]{0,1:T(8,128)} %reduce-scatter.8.cloned.1.call-done) | copy-start | bytes 98308
  639.0 141.0 %copy-start.1 = (bf16[8,1,64,768]{3,2,1,0:T(8,128)(2,1)S(1)}, bf16[8,1,64,768]{3,2,1,0:T(8,128)(2,1)}, u32[]{:S(2)}) copy-start(bf16[8,1,64,768]{3,2,1,0:T(8,128)(2,1)} %param.24) | copy-start | bytes 2359300
  (67 other events, 231.7 us)
Sparse Core Ops, SparseCore 0:
  10.8 49.3 all-gather.6
  62.3 27.2 all-gather.8
  91.8 28.8 all-gather.4
  359.2 27.7 reduce-scatter.11
  402.2 15.5 reduce-scatter.13
  420.2 58.3 reduce-scatter.9
  481.7 19.5 reduce-scatter.7
  504.6 70.4 all-reduce.19
  577.9 57.4 reduce-scatter.5
  641.4 132.9 all-reduce.21
where the time goes:
time: 792 us; the launch traced here: 787 us
  waiting for transfers between devices  344 us (43%)
  matrix products  158 us (20%)
  blocking collectives  113 us (14%)
  local copies, waits for them, and re-layouts  83.5 us (11%)
  other arithmetic  56.7 us (7%)
  between operations  18 us (2%)
  starting transfers between devices  13.7 us (2%)
    psum x1, waiting for transfers between devices, shards(): lax.psum((chosen[:, None, None] * indown_sum[None], chosen[:, None, None]...  134 us
    psum x1, waiting for transfers between devices, shards(): lax.psum((chosen[:, None, None, None] * inup_sum[None]).astype(jnp.bfloat...  70.8 us
    reduce_scatter x1, waiting for transfers between devices, shards(): lax.psum_scatter(jnp.dot(normed_out, full_out, preferred_element_type=jnp...  58.3 us
    dot_general x3, matrix products, state_mixer(): inside = jnp.einsum('ctsh,cshp->cthp', weights, block_x, precision=HIGHEST)  54.3 us
    reduce_scatter x1, waiting for transfers between devices, shards(): lax.psum_scatter(normed_part, 'tensor', scatter_dimension=0, tiled=True)  50.1 us
    unnamed x223, local copies, waits for them, and re-layouts  36.8 us
    all_gather x1, blocking collectives, shards(): lax.all_gather(w_out, 'dp', axis=1, tiled=True)  31.6 us
    all_gather x1, blocking collectives, shards(): lax.all_gather(w_bc, 'dp', axis=0, tiled=True)  31.3 us
  transfers between devices with their start and end apart: 12, of which 6 were waited for; matrix products, arithmetic and copies ran while one was open for 14% of the time, Pallas kernels for 0%

commit v1 on v0

--- a/solution.py
+++ b/solution.py
@@ -119,7 +119,10 @@
     placed = (dealt_to[None, :] == slot_ids[:, None]).astype(jnp.int32)
     seq_of = jnp.sum(placed * slot_ids[None, :], axis=1)
     picked = jnp.take(tokens, seq_of, axis=0)
-    arrived = lax.all_to_all(picked, "dp", split_axis=0, concat_axis=2, tiled=True)
+    arrived = jnp.concatenate(
+        lax.all_to_all(jnp.stack(jnp.split(picked, lax.axis_size("dp"), axis=0)), "dp", 0, 0),
+        axis=2,
+    )
     tok_rows = arrived.reshape(-1, model_dim)
     tok_dev = tok_rows.shape[0]
     group_id = lax.axis_index("dp")

time: 792 us -> 802 us (1.013)
    unnamed x223 -> x228, local copies, waits for them, and re-layouts: 36.8 us -> 41.5 us
  transfers between devices with their start and end apart: 12 -> 12, of which waited for: 6 -> 6; matrix products, arithmetic and copies ran while one was open for 14% -> 15% of each run, Pallas kernels for 0% -> 0%
where the time goes in v1:
time: 802 us; the launch traced here: 796 us
  waiting for transfers between devices  347 us (43%)
  matrix products  158 us (20%)
  blocking collectives  113 us (14%)
  local copies, waits for them, and re-layouts  88.8 us (11%)
  other arithmetic  57.3 us (7%)
  between operations  17.9 us (2%)
  starting transfers between devices  13.7 us (2%)
    psum x1, waiting for transfers between devices, shards(): lax.psum((chosen[:, None, None] * indown_sum[None], chosen[:, None, None]...  134 us
    psum x1, waiting for transfers between devices, shards(): lax.psum((chosen[:, None, None, None] * inup_sum[None]).astype(jnp.bfloat...  70.8 us
    reduce_scatter x1, waiting for transfers between devices, shards(): lax.psum_scatter(jnp.dot(normed_out, full_out, preferred_element_type=jnp...  58.3 us
    dot_general x3, matrix products, state_mixer(): inside = jnp.einsum('ctsh,cshp->cthp', weights, block_x, precision=HIGHEST)  54.3 us
    reduce_scatter x1, waiting for transfers between devices, shards(): lax.psum_scatter(normed_part, 'tensor', scatter_dimension=0, tiled=True)  50.4 us
    unnamed x228, local copies, waits for them, and re-layouts  41.5 us
    all_gather x1, blocking collectives, shards(): lax.all_gather(w_out, 'dp', axis=1, tiled=True)  31.6 us
    all_gather x1, blocking collectives, shards(): lax.all_gather(w_bc, 'dp', axis=0, tiled=True)  31.3 us
  transfers between devices with their start and end apart: 12, of which 6 were waited for; matrix products, arithmetic and copies ran while one was open for 15% of the time, Pallas kernels for 0%

profile of v1, /device:TPU:0, one launch (start us, length us, event | category | flops | bytes accessed | tf_op | source)
XLA Modules:
  0.0 796.4 jit_solution(10344706451945506515)
XLA Ops:
  23.0 7.4 all-to-all-start
  30.5 29.6 %all-to-all-done = bf16[8,1,1,64,768]{4,3,2,1,0:T(8,128)(2,1)S(1)} async-done(((bf16[8,1,1,64,768]{4,3,2,1,0:T(8,128)(2,1)}), bf16[8,1,1,64,768]{4,3,2,1,0:T(8,128)(2,1)S(1)}, u32[]{:S(2)}, u32[]{:S(2)}) %all-to-all-start) | async-done | bytes 786464 | tf_op jit(solution)/shard_map/all_to_all | solution.py:123
  64.7 26.0 %all-gather = bf16[8,96,6]{1,2,0:T(8,128)(2,1)S(1)} all-gather(bf16[1,96,6]{1,2,0:T(8,128)(2,1)S(1)} %bitcast.395), channel_id=1, replica_groups=mesh['dp'=8,'tensor'=4] {'dp'}, dimensions={0}, use_global_device_ids=true | all-gather | bytes 10368 | tf_op jit(solution)/shard_map/all_gather | solution.py:113
  93.9 5.8 all_gather.31
  101.5 31.3 %all_gather.27 = bf16[768,256]{1,0:T(8,128)(2,1)S(1)} all-gather(bf16[96,256]{1,0:T(8,128)(2,1)} %param.32), channel_id=1, replica_groups=mesh['dp'=8,'tensor'=4] {'dp'}, dimensions={0}, use_global_device_ids=true | all-gather | bytes 442368 | tf_op jit(solution)/shard_map/all_gather | solution.py:114
  134.7 31.6 %all_gather.29 = bf16[384,768]{0,1:T(8,128)(2,1)S(1)} all-gather(bf16[384,96]{0,1:T(8,128)(2,1)} %param.41), channel_id=1, replica_groups=mesh['dp'=8,'tensor'=4] {'dp'}, dimensions={1}, use_global_device_ids=true | all-gather | bytes 663552 | tf_op jit(solution)/shard_map/all_gather | solution.py:115
  166.6 5.9 all_gather.26
  174.8 5.4 fusion.231
  180.2 3.6 compare_select_fusion.2
  194.8 3.9 fusion.227
  199.8 3.0 fusion.223
  202.8 3.6 copy.303
  211.5 3.8 copy.304
  215.4 4.4 fusion.33
  219.7 4.0 copy.232
  223.7 3.5 copy.306
  229.1 3.8 fusion.41
  235.4 3.0 fusion.84
  238.5 15.3 %bitcast_add_fusion.2 = f32[8,256,6,64]{1,3,2,0:T(8,128)S(1)} fusion(f32[8,256,6,64]{1,3,2,0:T(8,128)S(1)} %fusion.84, f32[8,256,6]{1,2,0:T(8,128)S(1)} %bitcast.374, f32[8,256,6]{1,2,0:T(8,128)S(1)} %copy-done.64, f32[8,256,256]{2,1,0:T(8,128)S(1)} %fusion.229, pred[256,256]{1,0:T(8,128)(4,1)S(1)} %copy-done.65, f32[8,256,6,64]{1,0,3,2:T(8,128)S(1)} %bitcast.339, ...), kind=kOutput, calls=%fused_computation.50 | convolution fusion | flops 2433220608 | bytes 11747328 | tf_op jit(solution)/shard_map/jvp(ctsh,cshp->cthp)/dot_general | solution.py:44
  258.7 3.6 copy.248
  262.3 10.0 %multiply_reduce_fusion.3 = (f32[2048]{0:T(1024)}, f32[2048]{0:T(1024)}, f32[2048,384]{1,0:T(8,128)}, f32[2048,384]{1,0:T(8,128)}) fusion(f32[2048,1,384]{2,0,1:T(8,128)} %copy.304, f32[2048,384]{1,0:T(8,128)} %copy.248, f32[2048,384]{1,0:T(8,128)} %get-tuple-element.75, f32[384]{0:T(512)} %mul.549, f32[2048,384]{1,0:T(8,128)} %fusion.231, ...), kind=kOutput, calls=%fused_computation.55 | convolution fusion | flops 38531072 | bytes 19058692 | tf_op jit(solution)/shard_map/dot_general | solution.py:197
  272.2 12.8 %all-reduce.16 = (f32[2048]{0:T(1024)}, f32[2048]{0:T(1024)}) all-reduce(f32[2048]{0:T(1024)} %get-tuple-element.57, f32[2048]{0:T(1024)} %get-tuple-element.56), channel_id=1, replica_groups=mesh['dp'=8,'tensor'=4] {'tensor'}, use_global_device_ids=true, to_apply=%region_3.5 | all-reduce | flops 4096 | bytes 32768 | tf_op jit(solution)/shard_map/psum | solution.py:163
  286.4 9.0 %fusion.24 = (f32[2048,1,384]{2,0,1:T(8,128)}, f32[2048,384]{1,0:T(8,128)}, bf16[2048,384]{1,0:T(8,128)(2,1)}) fusion(f32[2048,1,384]{2,0,1:T(8,128)} %copy.304, f32[2048]{0:T(1024)S(1)} %broadcast_multiply_fusion.11, f32[2048,384]{1,0:T(8,128)} %get-tuple-element.73, f32[2048]{0:T(1024)S(1)} %get-tuple-element.93, f32[2048,384]{1,0:T(8,128)} %get-tuple-element.103, ...), kind=kLoop, calls=%fused_computation.34 | loop fusion | flops 19660800 | bytes 23620608 | tf_op jit(solution)/shard_map/transpose(jvp())/broadcast_in_dim | solution.py:82
  295.4 4.0 copy.250
  299.4 3.4 copy.309
  302.8 7.0 fusion.88
  309.9 3.8 fusion.76
  313.7 5.9 fusion.219
  322.1 7.0 fusion.91
  329.1 4.5 fusion.78
  334.4 24.8 %fusion.9 = (f32[8,256,6]{1,2,0:T(8,128)}, f32[8,256,6]{1,2,0:T(8,128)}, f32[8,256,6]{1,2,0:T(8,128)}, f32[8,256,256]{2,1,0:T(8,128)S(1)}) fusion(f32[8,256,6]{1,2,0:T(8,128)} %bitcast.372, f32[8,256,6]{1,2,0:T(8,128)} %copy.234, f32[8,256,256]{2,1,0:T(8,128)} %copy-done.32, pred[256,256]{1,0:T(8,128)(4,1)} %iota_compare_fusion, ...), kind=kOutput, calls=%fused_computation.14 | convolution fusion | flops 2462543872 | bytes 10797056 | tf_op jit(solution)/shard_map/transpose(jvp(ctsh,cshp->cthp))/dot_general | solution.py:44
  359.1 3.5 convolution_add_fusion.2
  368.3 14.2 %bitcast_add_fusion.1 = f32[8,256,6,64]{1,3,2,0:T(8,128)S(1)} fusion(f32[8,256,6,64]{1,3,2,0:T(8,128)} %fusion.78, f32[8,256,6]{1,2,0:T(8,128)} %bitcast.373, f32[8,256,6]{1,2,0:T(8,128)} %copy.234, f32[8,256,256]{2,1,0:T(8,128)} %copy-done.32, pred[256,256]{1,0:T(8,128)(4,1)} %iota_compare_fusion, f32[8,6,64,256]{3,0,2,1:T(8,128)} %bitcast.346, ...), kind=kOutput, calls=%fused_computation.43 | convolution fusion | flops 2433220608 | bytes 11747328 | tf_op jit(solution)/shard_map/transpose(jvp(ctsh,cshp->cthp))/dot_general | solution.py:44
  384.2 3.1 copy.310
  387.4 3.7 copy.257
  391.2 3.8 multiply_reduce_fusion.1
  396.9 4.3 multiply_reduce_fusion.2
  403.1 3.2 broadcast_multiply_fusion
  411.3 4.0 fusion.232
  415.3 3.8 bitcast_add_fusion
  429.1 4.5 fusion.230
  437.3 50.4 %reduce-scatter.10.cloned.1.call-done = f32[512,768]{1,0:T(8,128)} async-done(((f32[2048,768]{1,0:T(8,128)}), f32[512,768]{1,0:T(8,128)}) %reduce-scatter.10.cloned.1.call-update) | async-done | bytes 1572880 | tf_op jit(solution)/shard_map/reduce_scatter | solution.py:219
  493.3 6.5 reduce.12
  500.9 5.7 all-to-all-start.1
  506.6 3.9 reduce-scatter.8.cloned.1.call-done
  513.5 70.8 %all-reduce.20.cloned.1.call-done = bf16[8,16,2,384]{3,2,1,0:T(2,128)(2,1)} async-done(((bf16[8,16,2,384]{3,2,1,0:T(2,128)(2,1)}), bf16[8,16,2,384]{3,2,1,0:T(2,128)(2,1)}) %all-reduce.20.cloned.1.call-update) | async-done | bytes 196624 | tf_op jit(solution)/shard_map/psum | solution.py:248
  586.1 58.3 %reduce-scatter.6.cloned.1.call-done = f32[512,768]{1,0:T(8,128)} async-done(((f32[2048,768]{1,0:T(8,128)}), f32[512,768]{1,0:T(8,128)}) %reduce-scatter.6.cloned.1.call-update) | async-done | bytes 1572880 | tf_op jit(solution)/shard_map/reduce_scatter | solution.py:169
  649.7 133.8 %all-reduce.22.cloned.1.call-done = (f32[8,768,16]{1,2,0:T(8,128)}, f32[8,1536,16]{1,2,0:T(8,128)}, f32[8,16,768]{2,1,0:T(8,128)}) async-done(((f32[8,768,16]{1,2,0:T(8,128)}, f32[8,1536,16]{1,2,0:T(8,128)}, f32[8,16,768]{2,1,0:T(8,128)}), (f32[8,768,16]{1,2,0:T(8,128)}, f32[8,1536,16]{1,2,0:T(8,128)}, f32[8,16,768]{2,1,0:T(8,128)})) %all-reduce.22.cloned.1.call-update) | async-done | bytes 1572880 | tf_op jit(solution)/shard_map/psum | solution.py:240
  (347 shorter events, 110.4 us)
Async XLA Ops:
  7.2 9.6 %copy-start = (bf16[8,1,64,768]{3,2,1,0:T(8,128)(2,1)S(1)}, bf16[8,1,64,768]{3,2,1,0:T(8,128)(2,1)}, u32[]{:S(2)}) copy-start(bf16[8,1,64,768]{3,2,1,0:T(8,128)(2,1)} %param.24) | copy-start | bytes 2359300
  7.2 165.3 %all-gather.7.cloned.1.call-start = ((), (), s32[]{:S(2)}) async-start(), calls=%async_computation.8 | async-start | bytes 1327104 | tf_op jit(solution)/shard_map/all_gather | solution.py:112
  8.9 165.9 %all-gather.9.cloned.1.call-start = ((), (), s32[]{:S(2)}) async-start(), calls=%async_computation.11 | async-start | bytes 3932160 | tf_op jit(solution)/shard_map/all_gather | solution.py:194
  17.4 13.0 %copy-start.94 = (bf16[768]{0:T(1024)(128)(2,1)S(1)}, bf16[768]{0:T(1024)(128)(2,1)}, u32[]{:S(2)}) copy-start(bf16[768]{0:T(1024)(128)(2,1)} %param.29) | copy-start | bytes 4612
  22.1 40.0 %copy-start.101 = (s32[8]{0:T(128)S(1)}, s32[8]{0:T(128)}, u32[]{:S(2)}) copy-start(s32[8]{0:T(128)} %param.28) | copy-start | bytes 100
  22.1 41.2 %copy-start.98 = (bf16[384]{0:T(512)(128)(2,1)S(1)}, bf16[384]{0:T(512)(128)(2,1)}, u32[]{:S(2)}) copy-start(bf16[384]{0:T(512)(128)(2,1)} %param.40) | copy-start | bytes 2308
  22.1 41.8 %copy-start.99 = (f32[6]{0:T(128)S(1)}, f32[6]{0:T(128)}, u32[]{:S(2)}) copy-start(f32[6]{0:T(128)} %param.39) | copy-start | bytes 76
  22.1 42.6 %copy-start.95 = (bf16[96,6]{0,1:T(8,128)(2,1)S(1)}, bf16[96,6]{0,1:T(8,128)(2,1)}, u32[]{:S(2)}) copy-start(bf16[96,6]{0,1:T(8,128)(2,1)} %param.31) | copy-start | bytes 3460
  22.1 68.7 %copy-start.55 = (bf16[8,16,2,384]{3,2,1,0:T(2,128)(2,1)S(1)}, bf16[8,16,2,384]{3,2,1,0:T(2,128)(2,1)}, u32[]{:S(2)}) copy-start(bf16[8,16,2,384]{3,2,1,0:T(2,128)(2,1)} %param.43) | copy-start | bytes 589828
  22.1 69.5 %copy-start.56 = (bf16[8,768,16]{1,2,0:T(8,128)(2,1)S(1)}, bf16[8,768,16]{1,2,0:T(8,128)(2,1)}, u32[]{:S(2)}) copy-start(bf16[8,768,16]{1,2,0:T(8,128)(2,1)} %param.42) | copy-start | bytes 589828
  22.3 69.8 %copy-start.48 = (bf16[8,1536,16]{1,2,0:T(8,128)(2,1)S(1)}, bf16[8,1536,16]{1,2,0:T(8,128)(2,1)}, u32[]{:S(2)}) copy-start(bf16[8,1536,16]{1,2,0:T(8,128)(2,1)} %param.44) | copy-start | bytes 1179652
  23.0 70.4 %copy-start.57 = (bf16[8,16,768]{2,1,0:T(8,128)(2,1)S(1)}, bf16[8,16,768]{2,1,0:T(8,128)(2,1)}, u32[]{:S(2)}) copy-start(bf16[8,16,768]{2,1,0:T(8,128)(2,1)} %param.45) | copy-start | bytes 589828
  23.0 70.6 %copy-start.19 = (bf16[512,768]{1,0:T(8,128)(2,1)S(1)}, bf16[512,768]{1,0:T(8,128)(2,1)}, u32[]{:S(2)}) copy-start(bf16[512,768]{1,0:T(8,128)(2,1)} %fusion.62) | copy-start | bytes 2359300
  23.0 37.1 %all-to-all-start = ((bf16[8,1,1,64,768]{4,3,2,1,0:T(8,128)(2,1)}), bf16[8,1,1,64,768]{4,3,2,1,0:T(8,128)(2,1)S(1)}, u32[]{:S(2)}, u32[]{:S(2)}) async-start(bf16[8,1,1,64,768]{4,3,2,1,0:T(8,128)(2,1)} %fusion.141), calls=%async_computation | async-start | bytes 1572864 | tf_op jit(solution)/shard_map/all_to_all | solution.py:123
  30.4 69.9 %copy-start.90 = (f32[4,384]{1,0:T(4,128)S(1)}, f32[4,384]{1,0:T(4,128)}, u32[]{:S(2)}) copy-start(f32[4,384]{1,0:T(4,128)} %param.33) | copy-start | bytes 18436
  30.4 149.8 %all-gather.5.cloned.1.call-start = ((), (), s32[]{:S(2)}) async-start(), calls=%async_computation.7 | async-start | bytes 3932160 | tf_op jit(solution)/shard_map/all_gather | solution.py:149
  30.5 29.9 %copy-start.66 = (f32[768]{0:T(1024)}, f32[768]{0:T(1024)S(1)}, u32[]{:S(2)}) copy-start(f32[768]{0:T(1024)S(1)} %convert_element_type.108) | copy-start | bytes 9220
  60.0 40.9 %copy-start.5 = (bf16[8,1,1,64,768]{4,3,2,1,0:T(8,128)(2,1)}, bf16[8,1,1,64,768]{4,3,2,1,0:T(8,128)(2,1)S(1)}, u32[]{:S(2)}) copy-start(bf16[8,1,1,64,768]{4,3,2,1,0:T(8,128)(2,1)S(1)} %all-to-all-done) | copy-start | bytes 2359300
  60.3 73.8 %copy-start.91 = (f32[4,256]{1,0:T(4,128)S(1)}, f32[4,256]{1,0:T(4,128)}, u32[]{:S(2)}) copy-start(f32[4,256]{1,0:T(4,128)} %param.35) | copy-start | bytes 12292
  62.0 104.2 %copy-start.21 = (bf16[512,768]{1,0:T(8,128)(2,1)S(1)}, bf16[512,768]{1,0:T(8,128)(2,1)}, u32[]{:S(2)}) copy-start(bf16[512,768]{1,0:T(8,128)(2,1)} %fusion.67) | copy-start | bytes 2359300
  62.1 373.7 %reduce-scatter.12.cloned.1.call-start = ((), (), s32[]{:S(2)}) async-start(), calls=%async_computation.13 | async-start | bytes 2621440 | tf_op jit(solution)/shard_map/reduce_scatter | solution.py:221
  92.1 82.7 %copy-start.37 = (bf16[1,768,16]{2,1,0:T(8,128)(2,1)}, bf16[1,768,16]{2,1,0:T(8,128)(2,1)S(1)}, u32[]{:S(2)}) copy-start(bf16[1,768,16]{2,1,0:T(8,128)(2,1)S(1)} %copy.279) | copy-start | bytes 73732
  93.6 40.5 %copy-start.53 = (bf16[1,16,768]{2,0,1:T(2,128)(2,1)}, bf16[1,16,768]{2,0,1:T(2,128)(2,1)S(1)}, u32[]{:S(2)}) copy-start(bf16[1,16,768]{2,0,1:T(2,128)(2,1)S(1)} %fusion.135) | copy-start | bytes 73732
  166.3 14.0 %copy-start.30 = (bf16[384,768]{0,1:T(8,128)(2,1)}, bf16[384,768]{0,1:T(8,128)(2,1)S(1)}, u32[]{:S(2)}) copy-start(bf16[384,768]{0,1:T(8,128)(2,1)S(1)} %all_gather.29) | copy-start | bytes 1769476
  180.2 14.5 %copy-start.3 = (bf16[2048,768]{1,0:T(8,128)(2,1)S(1)}, bf16[2048,768]{1,0:T(8,128)(2,1)}, u32[]{:S(2)}) copy-start(bf16[2048,768]{1,0:T(8,128)(2,1)} %all-gather.5.cloned.1.call-done) | copy-start | bytes 9437188
  238.5 15.4 %copy-start.23 = (f32[8,256,6,64]{1,3,2,0:T(8,128)}, f32[8,256,6,64]{1,3,2,0:T(8,128)S(1)}, u32[]{:S(2)}) copy-start(f32[8,256,6,64]{1,3,2,0:T(8,128)S(1)} %fusion.84) | copy-start | bytes 9437188
  302.8 26.3 %copy-start.2 = (f32[48,8,8,256]{3,2,1,0:T(8,128)}, f32[48,8,8,256]{3,2,1,0:T(8,128)S(1)}, u32[]{:S(2)}) copy-start(f32[48,8,8,256]{3,2,1,0:T(8,128)S(1)} %copy.309) | copy-start | bytes 9437188
  334.4 24.8 %copy-start.14 = (f32[2048,128]{1,0:T(8,128)S(1)}, f32[2048,128]{1,0:T(8,128)}, u32[]{:S(2)}) copy-start(f32[2048,128]{1,0:T(8,128)} %get-tuple-element.90) | copy-start | bytes 3145732
  334.4 24.8 %copy-start.28 = (f32[8,256,128]{2,1,0:T(8,128)S(1)}, f32[8,256,128]{2,1,0:T(8,128)}, u32[]{:S(2)}) copy-start(f32[8,256,128]{2,1,0:T(8,128)} %fusion.91) | copy-start | bytes 3145732
  368.2 69.0 %reduce-scatter.14.cloned.1.call-start = ((), (), s32[]{:S(2)}) async-start(), calls=%async_computation.14 | async-start | bytes 163840 | tf_op jit(solution)/shard_map/reduce_scatter | solution.py:220
  411.2 76.5 %reduce-scatter.10.cloned.1.call-start = ((), (), s32[]{:S(2)}) async-start(), calls=%async_computation.12 | async-start | bytes 7864320 | tf_op jit(solution)/shard_map/reduce_scatter | solution.py:219
  419.1 91.3 %reduce-scatter.8.cloned.1.call-start = ((), (), s32[]{:S(2)}) async-start(), calls=%async_computation.10 | async-start | bytes 163840 | tf_op jit(solution)/shard_map/reduce_scatter | solution.py:175
  424.9 159.3 %all-reduce.20.cloned.1.call-start = ((), (), s32[]{:S(2)}) async-start(), calls=%async_computation.15 | async-start | bytes 393216 | tf_op jit(solution)/shard_map/psum | solution.py:248
  429.0 215.4 %reduce-scatter.6.cloned.1.call-start = ((), (), s32[]{:S(2)}) async-start(), calls=%async_computation.9 | async-start | bytes 7864320 | tf_op jit(solution)/shard_map/reduce_scatter | solution.py:169
  434.2 53.5 %copy-start.6 = (bf16[8,1,1,64,768]{4,3,2,1,0:T(8,128)(2,1)S(1)}, bf16[8,1,1,64,768]{4,3,2,1,0:T(8,128)(2,1)}, u32[]{:S(2)}) copy-start(bf16[8,1,1,64,768]{4,3,2,1,0:T(8,128)(2,1)} %copy-done.5) | copy-start | bytes 2359300
  434.2 53.5 %copy-start.67 = (f32[768]{0:T(1024)S(1)}, f32[768]{0:T(1024)}, u32[]{:S(2)}) copy-start(f32[768]{0:T(1024)} %copy-done.66) | copy-start | bytes 9220
  437.2 52.6 %copy-start.29 = (bf16[1,512,768]{2,1,0:T(8,128)(2,1)S(1)}, bf16[1,512,768]{2,1,0:T(8,128)(2,1)}, u32[]{:S(2)}) copy-start(bf16[1,512,768]{2,1,0:T(8,128)(2,1)} %param.25) | copy-start | bytes 2359300
  492.8 17.7 %copy-start.20 = (bf16[512,768]{1,0:T(8,128)(2,1)S(1)}, bf16[512,768]{1,0:T(8,128)(2,1)}, u32[]{:S(2)}) copy-start(bf16[512,768]{1,0:T(8,128)(2,1)} %fusion.62) | copy-start | bytes 2359300
  493.3 19.0 %copy-start.22 = (bf16[512,768]{1,0:T(8,128)(2,1)S(1)}, bf16[512,768]{1,0:T(8,128)(2,1)}, u32[]{:S(2)}) copy-start(bf16[512,768]{1,0:T(8,128)(2,1)} %fusion.67) | copy-start | bytes 2359300
  493.3 19.0 %copy-start.58 = (f32[512,16]{0,1:T(8,128)S(1)}, f32[512,16]{0,1:T(8,128)}, u32[]{:S(2)}) copy-start(f32[512,16]{0,1:T(8,128)} %reduce-scatter.14.cloned.1.call-done) | copy-start | bytes 98308
  500.8 12.6 %copy-start.96 = (s32[8]{0:T(128)S(1)}, s32[8]{0:T(128)}, u32[]{:S(2)}) copy-start(s32[8]{0:T(128)} %get-tuple-element.106) | copy-start | bytes 100
  500.8 12.6 %copy-start.100 = (s32[8]{0:T(128)S(1)}, s32[8]{0:T(128)}, u32[]{:S(2)}) copy-start(s32[8]{0:T(128)} %param.27) | copy-start | bytes 100
  500.8 143.6 %copy-start.54 = (bf16[1,16,768]{2,0,1:T(2,128)(2,1)S(1)}, bf16[1,16,768]{2,0,1:T(2,128)(2,1)}, u32[]{:S(2)}) copy-start(bf16[1,16,768]{2,0,1:T(2,128)(2,1)} %copy-done.53) | copy-start | bytes 73732
  500.8 143.6 %copy-start.78 = (f32[512]{0:T(512)S(1)}, f32[512]{0:T(512)}, u32[]{:S(2)}) copy-start(f32[512]{0:T(512)} %copy-done.77) | copy-start | bytes 6148
  500.9 146.3 %all-to-all-start.1 = ((bf16[8,2,24576]{2,1,0:T(2,128)(2,1)}), bf16[8,2,24576]{2,1,0:T(2,128)(2,1)S(1)}, u32[]{:S(2)}, u32[]{:S(2)}) async-start(bf16[8,2,24576]{2,1,0:T(2,128)(2,1)} %reshape.379), calls=%async_computation.6 | async-start | bytes 1572864 | tf_op jit(solution)/shard_map/all_to_all | solution.py:238
  506.5 277.0 %all-reduce.22.cloned.1.call-start = ((), (), s32[]{:S(2)}) async-start(), calls=%async_computation.16 | async-start | bytes 3145728 | tf_op jit(solution)/shard_map/psum | solution.py:240
  510.4 134.0 %copy-start.59 = (f32[512,16]{0,1:T(8,128)S(1)}, f32[512,16]{0,1:T(8,128)}, u32[]{:S(2)}) copy-start(f32[512,16]{0,1:T(8,128)} %reduce-scatter.8.cloned.1.call-done) | copy-start | bytes 98308
  648.1 141.1 %copy-start.1 = (bf16[8,1,64,768]{3,2,1,0:T(8,128)(2,1)S(1)}, bf16[8,1,64,768]{3,2,1,0:T(8,128)(2,1)}, u32[]{:S(2)}) copy-start(bf16[8,1,64,768]{3,2,1,0:T(8,128)(2,1)} %param.24) | copy-start | bytes 2359300
  (66 other events, 231.0 us)
Sparse Core Ops, SparseCore 0:
  10.8 49.8 all-gather.6
  62.8 27.9 all-gather.8
  93.0 28.5 all-gather.4
  368.3 27.7 reduce-scatter.11
  411.3 15.5 reduce-scatter.13
  429.3 58.3 reduce-scatter.9
  490.8 19.5 reduce-scatter.7
  513.7 70.4 all-reduce.19
  587.0 57.4 reduce-scatter.5
  650.5 132.9 all-reduce.21
